TPU v7x, 32 devices: a whole 2x2x4 slice. The times are simulated.
32 devices in a mesh: tp: 2 (over core), ep: 16 (over z, y, x).
Axes of the slice: x: 2, y: 2, z: 4, core: 2. Of those that a mesh axis runs over, the one named last changes fastest.
Arguments:
- tokens: bfloat16 [2048, 4096], P('ep', 'tp'), may hold values from -6 to 6
- expert_ids: int32 [2048, 8], P('ep'), may hold values from 0 to 15, all different within a row; in each aligned block of 128 rows (0 to 127, 128 to 255, ...) at most 128 rows name the same one
- route_weights: float32 [2048, 8], P('ep'), may hold values from 0.1 to 1
- gate_weight: bfloat16 [16, 4096, 1536], P('ep', None, 'tp'), may hold values from -0.09375 to 0.09375
- up_weight: bfloat16 [16, 4096, 1536], P('ep', None, 'tp'), may hold values from -0.09375 to 0.09375
- down_weight: bfloat16 [16, 1536, 4096], P('ep', 'tp'), may hold values from -0.15625 to 0.15625
- value_weight: float32 [4096], P('tp'), may hold values from -0.375 to 0.375
- sequence_ids: int32 [16, 128], P('ep'), may hold values from 0 to 3, never falling along the last dimension, each value on 1 to 64 neighbouring positions
Outputs:
- layer_output: bfloat16 [2048, 4096], P('ep', 'tp')
- rewards: float32 [16, 4], P('ep')
Inputs may be any that keep to these rules, and one draw needn't show every extreme that they name: `expert_ids`: each token names 8 different experts. Within each group's 128 rows no expert is named more than 128 times, a bound that some block reaches. `sequence_ids`: within each group the ids never fall, every one of the 4 ids occurs, and the longest sequence has exactly 64 tokens.
All inputs are finite; a program needn't handle non-finite values.
Results may differ from a plain program's by a relative error of at most 0.0095.
Values may be sent and summed in bfloat16 or wider, within the bound.
A program may use at most 128 MiB of HBM per device.

v0:
```python
import jax
import jax.numpy as jnp
from jax import lax
from jax.sharding import PartitionSpec as P

SEQ_GRP = 4


def slot_tables(route_ids, experts, capacity):
    tok_count, top_count = route_ids.shape
    flat_ids = route_ids.reshape(tok_count * top_count)
    one_hot = (flat_ids[:, None] == jnp.arange(experts, dtype=jnp.int32)[None, :]).astype(jnp.int32)
    before = jnp.cumsum(one_hot, axis=0, dtype=jnp.int32) - one_hot
    position = jnp.sum(before * one_hot, axis=1, dtype=jnp.int32)
    slot_index = flat_ids * capacity + position
    pair_token = jnp.arange(tok_count * top_count, dtype=jnp.int32) // top_count
    owner_token = jnp.zeros((experts * capacity,), jnp.int32).at[slot_index].set(pair_token)
    filled = jnp.zeros((experts * capacity,), jnp.int32).at[slot_index].set(1)
    return (slot_index.reshape(tok_count, top_count), owner_token, filled)


def shards(
    tokens,
    expert_ids,
    route_weights,
    gate_weight,
    up_weight,
    down_weight,
    value_weight,
    sequence_ids,
):
    tok_count, width_part = tokens.shape
    top_count = expert_ids.shape[1]
    groups = lax.axis_size("ep")
    capacity = min(tok_count, 2 * tok_count * top_count // groups)
    slot_index, owner_token, filled = slot_tables(expert_ids, groups, capacity)
    live_rows = filled.astype(jnp.bfloat16)[:, None]
    gate_local = gate_weight[0]
    up_local = up_weight[0]
    full_rows = lax.all_gather(tokens, "tp", axis=1, tiled=True)
    outgoing = (full_rows[owner_token] * live_rows).reshape(groups, capacity, full_rows.shape[1])
    arrived = lax.all_to_all(outgoing, "ep", split_axis=0, concat_axis=0, tiled=True)
    rows_in = arrived.reshape(groups * capacity, full_rows.shape[1])
    gate = jnp.dot(rows_in, gate_local, preferred_element_type=jnp.float32)
    upper = jnp.dot(rows_in, up_local, preferred_element_type=jnp.float32)
    hidden = (jax.nn.silu(gate) * upper).astype(jnp.bfloat16)
    terms = jnp.dot(hidden, down_weight[0], preferred_element_type=jnp.float32).astype(jnp.bfloat16)
    terms = terms.reshape(groups, capacity, terms.shape[1])
    summed = lax.psum_scatter(terms, "tp", scatter_dimension=2, tiled=True).astype(jnp.float32)
    expert_out = summed.astype(jnp.bfloat16)
    back_rows = lax.all_to_all(expert_out, "ep", split_axis=0, concat_axis=0, tiled=True)
    picked = back_rows.reshape(groups * capacity, width_part)[slot_index]
    share = route_weights / jnp.sum(route_weights, axis=1, keepdims=True)
    combined = tokens.astype(jnp.float32) + jnp.einsum(
        "tk,tkd->td", share, picked.astype(jnp.float32)
    )
    layer_output = combined.astype(jnp.bfloat16)
    as_float = layer_output.astype(jnp.float32)
    squares = jnp.sum(as_float * as_float, axis=1)
    along = jnp.sum(as_float * value_weight[None, :], axis=1)
    squares, along = lax.psum((squares, along), "tp")
    values = along * lax.rsqrt(squares / (width_part * lax.axis_size("tp")) + 1e-06)
    members = (sequence_ids[0][None, :] == jnp.arange(SEQ_GRP, dtype=jnp.int32)[:, None]).astype(
        jnp.float32
    )
    sums = jnp.sum(members * values[None, :], axis=1)
    counts = jnp.sum(members, axis=1)
    rewards = sums / counts
    return (layer_output, rewards[None, :])


def solution(mesh):
    in_specs = (
        P("ep", "tp"),
        P("ep", None),
        P("ep", None),
        P("ep", None, "tp"),
        P("ep", None, "tp"),
        P("ep", "tp", None),
        P("tp"),
        P("ep", None),
    )
    out_specs = (P("ep", "tp"), P("ep", None))
    return jax.shard_map(shards, mesh=mesh, in_specs=in_specs, out_specs=out_specs, check_vma=False)
```

profile of v0, /device:TPU:29, one launch (start us, length us, event | category | flops | bytes accessed | tf_op | source)
XLA Modules:
  0.0 736.1 jit_solution(15373931978590851427)
XLA Ops:
  7.2 0.0 all-gather.2.cloned.1.call-start
  7.2 0.7 all-gather.2.cloned.1.call-update
  7.9 0.0 reduce-scatter.2.cloned.1.call-start
  7.9 0.8 copy.17
  8.7 0.1 eq.44
  8.8 0.1 eq.40
  8.9 4.5 reduce-window.6
  13.5 0.1 slice.12
  13.5 0.1 copy.20
  13.7 0.1 copy.21
  13.8 0.1 broadcast_add_fusion
  13.9 0.1 reduce_sum.61
  14.0 0.1 mul.62
  14.1 4.3 scatter_custom_fusion
  18.5 4.3 scatter_custom_fusion.1
  22.8 0.0 all-gather.2.cloned.1.call-done
  22.9 30.0 %gather_fusion = bf16[2048,4096]{1,0:T(8,128)(2,1)} fusion(bf16[128,4096]{1,0:T(8,128)(2,1)} %all-gather.2.cloned.1.call-done, s32[2048]{0:T(1024)S(1)} %fusion.16), kind=kCustom, calls=%fused_computation | custom fusion | bytes 33562624 | tf_op jit(solution)/shard_map/gather | solution.py:41
  52.9 8.3 %broadcast_multiply_fusion = bf16[16,128,4096]{2,1,0:T(8,128)(2,1)S(1)} fusion(bf16[16,128,4096]{2,1,0:T(8,128)(2,1)} %bitcast.54, bf16[16,128]{1,0:T(8,128)(2,1)S(1)} %convert_bitcast_fusion), kind=kLoop, calls=%fused_computation.5 | loop fusion | flops 8388608 | bytes 33558528 | tf_op jit(solution)/shard_map/mul | solution.py:41
  61.2 0.0 copy-start.4
  61.2 367.4 %all_to_all.10 = bf16[16,128,4096]{2,1,0:T(8,128)(2,1)S(1)} all-to-all(bf16[16,128,4096]{2,1,0:T(8,128)(2,1)S(1)} %broadcast_multiply_fusion), channel_id=1, replica_groups=mesh['tp'=2,'ep'=16] {'ep'}, dimensions={0} | all-to-all | bytes 33554432 | tf_op jit(solution)/shard_map/all_to_all | solution.py:42
  428.6 0.0 copy-done.4
  428.6 15.0 %fusion.3 = f32[2048,768]{1,0:T(8,128)} fusion(bf16[2048,4096]{1,0:T(8,128)(2,1)S(1)} %bitcast.56, bf16[1,4096,768]{2,1,0:T(8,128)(2,1)S(1)} %copy-done.4), kind=kOutput, calls=%fused_computation.9 | convolution fusion | flops 12884901888 | bytes 29360128 | tf_op jit(solution)/shard_map/dot_general | solution.py:44
  443.6 19.2 %multiply_convert_fusion = bf16[2048,768]{1,0:T(8,128)(2,1)} fusion(f32[2048,768]{1,0:T(8,128)} %fusion.3, bf16[2048,4096]{1,0:T(8,128)(2,1)S(1)} %bitcast.57, bf16[1,4096,768]{2,1,0:T(8,128)(2,1)} %param.12), kind=kOutput, calls=%fused_computation.11 | convolution fusion | flops 12894339072 | bytes 32505856 | tf_op jit(solution)/shard_map/dot_general | solution.py:45
  462.8 19.5 %convolution_convert_fusion = bf16[2048,4096]{1,0:T(8,128)(2,1)} fusion(bf16[2048,768]{1,0:T(8,128)(2,1)} %multiply_convert_fusion, bf16[1,768,4096]{2,1,0:T(8,128)(2,1)} %param.13), kind=kOutput, calls=%fused_computation.4 | convolution fusion | flops 12893290496 | bytes 26214400 | tf_op jit(solution)/shard_map/dot_general | solution.py:47
  482.3 0.0 reduce-scatter.2.cloned.1.call-update
  482.3 0.0 copy-start.1
  482.3 28.0 %reduce-scatter.2.cloned.1.call-done = bf16[16,128,2048]{2,1,0:T(8,128)(2,1)} async-done(((bf16[16,128,4096]{2,1,0:T(8,128)(2,1)}), bf16[16,128,2048]{2,1,0:T(8,128)(2,1)}) %reduce-scatter.2.cloned.1.call-update) | async-done | bytes 8388624 | tf_op jit(solution)/shard_map/reduce_scatter | solution.py:49
  510.3 6.4 all-to-all-start.1
  516.7 0.1 reshape.98
  516.8 0.0 copy-done.1
  516.8 0.1 copy.22
  517.0 190.1 %all-to-all-done.1 = bf16[16,128,2048]{2,1,0:T(8,128)(2,1)} async-done(((bf16[16,128,2048]{2,1,0:T(8,128)(2,1)}), bf16[16,128,2048]{2,1,0:T(8,128)(2,1)}, u32[]{:S(2)}, u32[]{:S(2)}) %all-to-all-start.1) | async-done | bytes 8388640 | tf_op jit(solution)/shard_map/all_to_all | solution.py:51
  707.1 0.0 copy-start
  707.1 0.0 copy-start.2
  707.1 13.3 %gather_fusion.1 = bf16[1024,2048]{1,0:T(8,128)(2,1)} fusion(bf16[2048,2048]{1,0:T(8,128)(2,1)} %bitcast.12, s32[1024]{0:T(1024)S(1)} %broadcast_clamp_fusion), kind=kCustom, calls=%fused_computation.1 | custom fusion | bytes 8392704 | tf_op jit(solution)/shard_map/gather | solution.py:52
  720.4 0.0 copy-start.3
  720.4 3.4 fusion.7
  723.8 0.0 copy-done
  723.9 0.0 copy-done.2
  723.9 1.1 fusion.10
  725.0 3.5 all-reduce
  728.5 0.0 copy-done.3
  728.5 0.1 convert_reduce_fusion
  728.7 0.5 divide_bitcast_fusion.1
  (14 shorter events, 0.1 us)
Async XLA Ops:
  7.2 15.7 %all-gather.2.cloned.1.call-start = ((), (), s32[]{:S(2)}) async-start(), calls=%async_computation.3 | async-start | bytes 1572864 | tf_op jit(solution)/shard_map/all_gather | solution.py:40
  7.9 502.5 %reduce-scatter.2.cloned.1.call-start = ((), (), s32[]{:S(2)}) async-start(), calls=%async_computation.4 | async-start | bytes 25165824 | tf_op jit(solution)/shard_map/reduce_scatter | solution.py:49
  61.2 367.5 %copy-start.4 = (bf16[1,4096,768]{2,1,0:T(8,128)(2,1)S(1)}, bf16[1,4096,768]{2,1,0:T(8,128)(2,1)}, u32[]{:S(2)}) copy-start(bf16[1,4096,768]{2,1,0:T(8,128)(2,1)} %param.11) | copy-start | bytes 18874372
  482.3 34.5 %copy-start.1 = (f32[128,8]{0,1:T(8,128)S(1)}, f32[128,8]{0,1:T(8,128)}, u32[]{:S(2)}) copy-start(f32[128,8]{0,1:T(8,128)} %param.10) | copy-start | bytes 12292
  510.3 196.7 %all-to-all-start.1 = ((bf16[16,128,2048]{2,1,0:T(8,128)(2,1)}), bf16[16,128,2048]{2,1,0:T(8,128)(2,1)}, u32[]{:S(2)}, u32[]{:S(2)}) async-start(bf16[16,128,2048]{2,1,0:T(8,128)(2,1)} %reduce-scatter.2.cloned.1.call-done), calls=%async_computation.2 | async-start | bytes 16777216 | tf_op jit(solution)/shard_map/all_to_all | solution.py:51
  707.1 16.8 %copy-start = (bf16[128,2048]{1,0:T(8,128)(2,1)S(1)}, bf16[128,2048]{1,0:T(8,128)(2,1)}, u32[]{:S(2)}) copy-start(bf16[128,2048]{1,0:T(8,128)(2,1)} %param.8) | copy-start | bytes 1572868
  707.1 16.8 %copy-start.2 = (f32[2048]{0:T(1024)S(1)}, f32[2048]{0:T(1024)}, u32[]{:S(2)}) copy-start(f32[2048]{0:T(1024)} %param.14) | copy-start | bytes 24580
  720.4 8.1 %copy-start.3 = (s32[1,128]{1,0:T(1,128)S(1)}, s32[1,128]{1,0:T(1,128)}, u32[]{:S(2)}) copy-start(s32[1,128]{1,0:T(1,128)} %param.15) | copy-start | bytes 1540
Sparse Core Ops, SparseCore 0:
  9.5 10.6 all-gather.1
  482.4 27.8 reduce-scatter.1
where the time goes:
time: 736 us
  blocking collectives  371 us (50%)
  waiting for transfers between devices  219 us (30%)
  matrix products  57.1 us (8%)
  local copies, waits for them, and re-layouts  53.7 us (7%)
  other arithmetic  14.8 us (2%)
  between operations  14.2 us (2%)
    all_to_all x1, blocking collectives, shards(): lax.all_to_all(outgoing, 'ep', split_axis=0, concat_axis=0, tiled=True)  367 us
    all_to_all x1, waiting for transfers between devices, shards(): lax.all_to_all(expert_out, 'ep', split_axis=0, concat_axis=0, tiled=True)  190 us
    gather x1, local copies, waits for them, and re-layouts, shards(): full_rows[owner_token] * live_rows  30 us
    reduce_scatter x1, waiting for transfers between devices, shards(): lax.psum_scatter(terms, 'tp', scatter_dimension=2, tiled=True)  28 us
    dot_general x1, matrix products, shards(): jnp.dot(hidden, down_weight[0], preferred_element_type=jnp.float32)  19.5 us
    dot_general x1, matrix products, shards(): upper = jnp.dot(rows_in, up_local, preferred_element_type=jnp.float32)  19.2 us
    dot_general x1, matrix products, shards(): gate = jnp.dot(rows_in, gate_local, preferred_element_type=jnp.float32)  15 us
  transfers between devices with their start and end apart: 3, of which 2 were waited for; matrix products, arithmetic and copies ran while one was open for 2% of the time, Pallas kernels for 0%

commit v1 on v0

v1 whole, which is shorter than its diff:
```python
import jax
import jax.numpy as jnp
from jax import lax
from jax.experimental import pallas as pl
from jax.experimental.pallas import tpu as pltpu
from jax.sharding import PartitionSpec as P

SEQ_GRP = 4
CHUNKS = 1


def head(layer_output, value_weight, sequence_ids, parts):
    width_part = layer_output.shape[1]
    as_float = layer_output.astype(jnp.float32)
    squares = jnp.sum(as_float * as_float, axis=1)
    along = jnp.sum(as_float * value_weight[None, :], axis=1)
    squares, along = lax.psum((squares, along), "tp")
    values = along * lax.rsqrt(squares / (width_part * parts) + 1e-06)
    members = (sequence_ids[0][None, :] == jnp.arange(SEQ_GRP, dtype=jnp.int32)[:, None]).astype(
        jnp.float32
    )
    sums = jnp.sum(members * values[None, :], axis=1)
    counts = jnp.sum(members, axis=1)
    rewards = sums / counts
    return rewards[None, :]


def plain_shards(
    tokens,
    expert_ids,
    route_weights,
    gate_weight,
    up_weight,
    down_weight,
    value_weight,
    sequence_ids,
):
    tok_count, width_part = tokens.shape
    groups = lax.axis_size("ep")
    parts = lax.axis_size("tp")
    share = route_weights / jnp.sum(route_weights, axis=1, keepdims=True)
    named = expert_ids[:, :, None] == jnp.arange(groups, dtype=jnp.int32)[None, None, :]
    dense = jnp.sum(jnp.where(named, share[:, :, None], 0.0), axis=1)
    dense_all = lax.all_gather(dense, "ep", axis=0)
    mine = lax.dynamic_index_in_dim(dense_all, lax.axis_index("ep"), 2, keepdims=False)
    gate_local = gate_weight[0].reshape(parts, width_part, -1)
    up_local = up_weight[0].reshape(parts, width_part, -1)
    rows = tok_count // CHUNKS
    pieces = []
    for c in range(CHUNKS):
        own = tokens[c * rows:(c + 1) * rows]
        half = lax.all_gather(own, "ep", axis=0, tiled=True)
        full = lax.all_gather(half, "tp", axis=0)
        gate = jnp.einsum("qtd,qdf->tf", full, gate_local, preferred_element_type=jnp.float32)
        upper = jnp.einsum("qtd,qdf->tf", full, up_local, preferred_element_type=jnp.float32)
        scale = mine[:, c * rows:(c + 1) * rows].reshape(groups * rows, 1)
        hidden = (jax.nn.silu(gate) * upper).astype(jnp.bfloat16)
        terms = jnp.dot(hidden, down_weight[0], preferred_element_type=jnp.float32)
        terms = (terms * scale).astype(jnp.bfloat16)
        summed = lax.psum_scatter(terms, "tp", scatter_dimension=1, tiled=True)
        pieces.append(lax.psum_scatter(summed, "ep", scatter_dimension=0, tiled=True))
    routed = jnp.concatenate(pieces, axis=0).astype(jnp.float32)
    layer_output = (tokens.astype(jnp.float32) + routed).astype(jnp.bfloat16)
    return (layer_output, head(layer_output, value_weight, sequence_ids, parts))


MESH = pl.DeviceIdType.MESH
GRP = 128
PAD = 128


def fused(
    tok, gate_hbm, up_hbm, down_hbm, out,
    held, gate_w, up_w, down_w, hid, scale, part, s_in, f_in, z_in,
    w_sem, az_s, az_r, af_s, af_r, as_s, as_r, at_s, at_r,
    rt_s, rt_r, rs_s, rs_r, rf_s, rf_r, rz_s, rz_r,
):
    half = out.shape[1]
    t = lax.axis_index("tp")
    e = lax.axis_index("ep")
    x = lax.rem(e, 2)
    y = lax.rem(lax.div(e, 2), 2)
    z = lax.div(e, 4)
    l_own = lax.rem(e, 4)
    l_x = l_own + 1 - 2 * x
    l_y = l_own + 2 - 4 * y
    l_diag = 3 - l_own
    e_x = e + 1 - 2 * x
    e_y = e + 2 - 4 * y
    e_f = e_y * (1 - t) + e_x * t
    e_s = e_x * (1 - t) + e_y * t
    l_f = l_y * (1 - t) + l_x * t
    l_s = l_x * (1 - t) + l_y * t
    lines = (l_own, l_x, l_y, l_diag)
    i_f = 2 - t
    i_s = 1 + t
    near = (t, e_f)
    far = (t, e_s)
    twin = (1 - t, e)

    def peer(d):
        return (t, lax.rem(z + d, 4) * 4 + l_own)

    def span(d):
        return pl.ds(pl.multiple_of(lax.rem(z - d + 4, 4) * GRP, GRP), GRP)

    def remote(src, dst, send, recv, target):
        return pltpu.make_async_remote_copy(
            src_ref=src, dst_ref=dst, send_sem=send, recv_sem=recv,
            device_id=target, device_id_type=MESH,
        )

    loads = [
        pltpu.make_async_copy(a, b, w_sem.at[i])
        for i, (a, b) in enumerate(((gate_hbm, gate_w), (up_hbm, up_w), (down_hbm, down_w)))
    ]
    for load in loads:
        load.start()

    barrier = pltpu.get_barrier_semaphore()
    for target in (peer(1), peer(2), peer(3), near, far, twin):
        pl.semaphore_signal(barrier, inc=1, device_id=target, device_id_type=MESH)
    pl.semaphore_wait(barrier, 6)

    def own_block(d):
        return tok if d == 0 else held.at[t, l_own, span(d)]

    def z_copy(d):
        return remote(tok, held.at[t, l_own, span(0)], az_s.at[d - 1], az_r.at[d - 1], peer(d))

    def f_copy(d):
        return remote(own_block(d), held.at[t, l_own, span(d)], af_s.at[d], af_r.at[d], near)

    def s_copy(k, d):
        line = l_own if k == 0 else l_f
        src = own_block(d) if k == 0 else held.at[t, line, span(d)]
        return remote(src, held.at[t, line, span(d)], as_s.at[k, d], as_r.at[k, d], far)

    def t_copy(i, line, d, src=None):
        src = held.at[t, line, span(d)] if src is None else src
        return remote(src, held.at[t, line, span(d)], at_s.at[i, d], at_r.at[i, d], twin)

    def arrived(line, d, sem, core=None):
        ref = held.at[t if core is None else core, line, span(d)]
        remote(ref, ref, w_sem.at[0], sem, twin).wait_recv()

    sent = []

    def go(copy):
        copy.start()
        sent.append(copy)

    for d in (1, 3, 2):
        go(z_copy(d))
    go(f_copy(0))
    go(s_copy(0, 0))
    go(t_copy(0, l_own, 0, tok))
    held[t, l_own, span(0)] = tok[...]
    for d in (0, 1, 3, 2):
        if d:
            arrived(l_own, d, az_r.at[d - 1])
            go(f_copy(d))
            go(s_copy(0, d))
            go(t_copy(0, l_own, d))
        arrived(l_f, d, af_r.at[d])
        go(s_copy(1, d))
        go(t_copy(i_f, l_f, d))

    def expert(i):
        line = lines[i]
        for d in range(4):
            arrived(line, d, at_r.at[i, d], 1 - t)
        lane = lax.broadcasted_iota(jnp.int32, (4 * GRP, PAD), 1)
        shares = held[t, line, :, pl.ds(half, PAD)].astype(jnp.float32)
        scale[...] = jnp.sum(jnp.where(lax.rem(lane, 16) == e, shares, 0.0), axis=1, keepdims=True)

        def hidden(n, carry):
            cols = pl.ds(pl.multiple_of(n * 256, 256), 256)
            a = held[0, line, :, pl.ds(0, half)]
            b = held[1, line, :, pl.ds(0, half)]
            f32 = jnp.float32
            g = jnp.dot(a, gate_w[pl.ds(0, half), cols], preferred_element_type=f32)
            g += jnp.dot(b, gate_w[pl.ds(half, half), cols], preferred_element_type=f32)
            u = jnp.dot(a, up_w[pl.ds(0, half), cols], preferred_element_type=f32)
            u += jnp.dot(b, up_w[pl.ds(half, half), cols], preferred_element_type=f32)
            hid[:, cols] = (g / (1.0 + jnp.exp(-g)) * u * scale[...]).astype(jnp.bfloat16)
            return carry

        lax.fori_loop(0, hid.shape[1] // 256, hidden, 0)

        def term(n, core):
            cols = pl.ds(pl.multiple_of(core * half + n * 256, 256), 256)
            return jnp.dot(hid[...], down_w[:, cols], preferred_element_type=jnp.float32)

        def swap(c):
            cols = pl.ds(c * (half // 2), half // 2)
            return remote(
                held.at[1 - t, line, :, cols], part.at[i, :, cols],
                rt_s.at[i, c], rt_r.at[i, c], twin,
            )

        steps = half // 512
        for c in range(2):
            def other(n, carry):
                cols = pl.ds(pl.multiple_of(n * 256, 256), 256)
                held[1 - t, line, :, cols] = term(n, 1 - t).astype(jnp.bfloat16)
                return carry

            lax.fori_loop(c * steps, (c + 1) * steps, other, 0)
            go(swap(c))
        for c in range(2):
            swap(c).wait_recv()

            def mine(n, carry):
                cols = pl.ds(pl.multiple_of(n * 256, 256), 256)
                total = term(n, t) + part[i, :, cols].astype(jnp.float32)
                part[i, :, cols] = total.astype(jnp.bfloat16)
                return carry

            lax.fori_loop(c * steps, (c + 1) * steps, mine, 0)

    def rs_copy(k, d):
        i = i_s if k == 0 else 3
        return remote(part.at[i, span(d)], s_in.at[k, span(d)], rs_s.at[k, d], rs_r.at[k, d], far)

    def send_far(k):
        for d in (1, 3, 2, 0):
            rs_copy(k, d).start()

    for load in loads:
        load.wait()
    expert(0)
    for d in (0, 1, 3, 2):
        arrived(l_s, d, as_r.at[0, d])
        go(t_copy(i_s, l_s, d))
    expert(1)
    pl.when(t == 0)(lambda: send_far(0))
    for d in (0, 1, 3, 2):
        arrived(l_diag, d, as_r.at[1, d])
        go(t_copy(3, l_diag, d))
    expert(2)
    pl.when(t == 1)(lambda: send_far(0))
    expert(3)
    send_far(1)

    def add(dst, row, *others):
        def chunk(r, carry):
            at = pl.ds(pl.multiple_of(row + r * 16, 16), 16)
            total = dst[at].astype(jnp.float32)
            for other in others:
                total += other[at].astype(jnp.float32)
            dst[at] = total.astype(jnp.bfloat16)
            return carry

        lax.fori_loop(0, GRP // 16, chunk, 0)

    def start_row(d):
        return lax.rem(z - d + 4, 4) * GRP

    def rf_copy(d):
        return remote(part.at[i_f, span(d)], f_in.at[span(d)], rf_s.at[d], rf_r.at[d], near)

    def rz_copy(d):
        return remote(
            part.at[0, span(d)], z_in.at[d - 1], rz_s.at[d - 1], rz_r.at[d - 1], peer(4 - d)
        )

    for d in (1, 3, 2, 0):
        rs_copy(1, d).wait_recv()
        add(part.at[i_f], start_row(d), s_in.at[1])
        go(rf_copy(d))
    for d in (1, 3, 2, 0):
        rs_copy(0, d).wait_recv()
        rf_copy(d).wait_recv()
        add(part.at[0], start_row(d), s_in.at[0], f_in)
        if d:
            go(rz_copy(d))
    for d in (1, 3, 2):
        rz_copy(d).wait_recv()

    def last(r, carry):
        at = pl.ds(pl.multiple_of(r * 16, 16), 16)
        total = part[0, pl.ds(pl.multiple_of(z * GRP + r * 16, 16), 16)].astype(jnp.float32)
        for k in range(3):
            total += z_in[k, at].astype(jnp.float32)
        total += tok[at, pl.ds(0, half)].astype(jnp.float32)
        out[at] = total.astype(jnp.bfloat16)
        return carry

    lax.fori_loop(0, GRP // 16, last, 0)
    for copy in sent:
        copy.wait_send()
    for k in range(2):
        for d in range(4):
            rs_copy(k, d).wait_send()


def routed_layer(block, gate, up, down):
    half = block.shape[1] - PAD
    width, units = gate.shape
    bf16 = jnp.bfloat16
    dma = pltpu.SemaphoreType.DMA
    flops = 2 * 16 * GRP * 3 * width * units
    return pl.pallas_call(
        fused,
        out_shape=jax.ShapeDtypeStruct((GRP, half), bf16),
        in_specs=[pl.BlockSpec(memory_space=pltpu.VMEM)] + [pl.BlockSpec(memory_space=pl.ANY)] * 3,
        out_specs=pl.BlockSpec(memory_space=pltpu.VMEM),
        scratch_shapes=[
            pltpu.VMEM((2, 4, 4 * GRP, half + PAD), bf16),
            pltpu.VMEM((width, units), bf16),
            pltpu.VMEM((width, units), bf16),
            pltpu.VMEM((units, width), bf16),
            pltpu.VMEM((4 * GRP, units), bf16),
            pltpu.VMEM((4 * GRP, 1), jnp.float32),
            pltpu.VMEM((4, 4 * GRP, half), bf16),
            pltpu.VMEM((2, 4 * GRP, half), bf16),
            pltpu.VMEM((4 * GRP, half), bf16),
            pltpu.VMEM((3, GRP, half), bf16),
            dma((3,)),
            dma((3,)), dma((3,)),
            dma((4,)), dma((4,)),
            dma((2, 4)), dma((2, 4)),
            dma((4, 4)), dma((4, 4)),
            dma((4, 2)), dma((4, 2)),
            dma((2, 4)), dma((2, 4)),
            dma((4,)), dma((4,)),
            dma((3,)), dma((3,)),
        ],
        compiler_params=pltpu.CompilerParams(
            collective_id=0, has_side_effects=True, vmem_limit_bytes=63 * 1024 * 1024
        ),
        cost_estimate=pl.CostEstimate(
            flops=flops, bytes_accessed=6 * width * units, transcendentals=16 * GRP * units
        ),
    )(block, gate, up, down)


def shards(
    tokens,
    expert_ids,
    route_weights,
    gate_weight,
    up_weight,
    down_weight,
    value_weight,
    sequence_ids,
):
    tok_count, width_part = tokens.shape
    groups = lax.axis_size("ep")
    parts = lax.axis_size("tp")
    share = route_weights / jnp.sum(route_weights, axis=1, keepdims=True)
    named = expert_ids[:, :, None] == jnp.arange(groups, dtype=jnp.int32)[None, None, :]
    dense = jnp.sum(jnp.where(named, share[:, :, None], 0.0), axis=1)
    columns = []
    rest = dense
    for _ in range(3):
        top = lax.reduce_precision(rest, 8, 7)
        columns.append(top.astype(jnp.bfloat16))
        rest = rest - top
    blank = jnp.zeros((tok_count, PAD - 3 * groups), jnp.bfloat16)
    block = jnp.concatenate([tokens] + columns + [blank], axis=1)
    layer_output = routed_layer(block, gate_weight[0], up_weight[0], down_weight[0])
    return (layer_output, head(layer_output, value_weight, sequence_ids, parts))


def solution(mesh):
    in_specs = (
        P("ep", "tp"),
        P("ep", None),
        P("ep", None),
        P("ep", None, "tp"),
        P("ep", None, "tp"),
        P("ep", "tp", None),
        P("tp"),
        P("ep", None),
    )
    out_specs = (P("ep", "tp"), P("ep", None))
    body = shards if dict(mesh.shape) == {"tp": 2, "ep": 16} else plain_shards
    return jax.shard_map(body, mesh=mesh, in_specs=in_specs, out_specs=out_specs, check_vma=False)
```

time: 736 us -> 232 us (0.32)
  the two profiles are of different devices: /device:TPU:29 before, /device:TPU:0 now
where the time goes in v1:
time: 232 us
  Pallas kernels  213 us (92%)
  blocking collectives  10.3 us (4%)
  other arithmetic  4.11 us (2%)
  local copies, waits for them, and re-layouts  4.06 us (2%)
    pallas_call x1, Pallas kernels, routed_layer(): pl.pallas_call(fused, out_shape=jax.ShapeDtypeStruct((GRP, half), bf16),...  213 us
    psum x1, blocking collectives, head(): squares, along = lax.psum((squares, along), 'tp')  10.3 us

profile of v1, /device:TPU:0, one launch (start us, length us, event | category | flops | bytes accessed | tf_op | source)
XLA Modules:
  0.0 231.9 jit_solution(9674857014563900098)
XLA Ops:
  0.6 0.7 reduce_sum.54
  1.3 0.7 broadcast_divide_fusion
  2.0 0.7 select_reduce_fusion
  2.7 0.1 copy.16
  2.9 0.1 copy.15
  3.0 0.1 copy.14
  3.1 1.8 concatenate.3.tok
  5.0 0.0 copy-start
  5.0 0.0 copy-start.1
  5.0 212.8 %shard_map.95 = bf16[128,2048]{1,0:T(8,128)(2,1)} custom-call(bf16[128,2176]{1,0:T(8,128)(2,1)} %concatenate.3.tok, bf16[4096,768]{1,0:T(8,128)(2,1)} %bitcast.7, bf16[4096,768]{1,0:T(8,128)(2,1)} %bitcast.8, bf16[768,4096]{1,0:T(8,128)(2,1)} %bitcast.9), custom_call_target="tpu_custom_call" | custom-call | flops 38654705664 | bytes 18874368 | tf_op jit(solution)/shard_map/pallas_call | solution.py:304
  217.8 0.0 copy-done
  217.8 1.3 fusion.1
  219.1 10.3 %all-reduce = (f32[128]{0:T(128)S(1)}, f32[128]{0:T(128)S(1)}) all-reduce(f32[128]{0:T(128)S(1)} %get-tuple-element.3, f32[128]{0:T(128)S(1)} %get-tuple-element.2), channel_id=1, replica_groups=mesh['tp'=2,'ep'=16] {'tp'}, use_global_device_ids=true, to_apply=%region_3.4 | all-reduce | flops 256 | bytes 2048 | tf_op jit(solution)/shard_map/psum | solution.py:17
  229.4 0.0 copy-done.1
  229.4 0.1 convert_reduce_fusion
  229.5 0.5 divide_bitcast_fusion
  230.1 1.9 copy.18
  (4 shorter events, 0.0 us)
Async XLA Ops:
  5.0 212.8 %copy-start = (f32[2048]{0:T(1024)S(1)}, f32[2048]{0:T(1024)}, u32[]{:S(2)}) copy-start(f32[2048]{0:T(1024)} %param.14) | copy-start | bytes 24580
  5.0 224.4 %copy-start.1 = (s32[1,128]{1,0:T(1,128)S(1)}, s32[1,128]{1,0:T(1,128)}, u32[]{:S(2)}) copy-start(s32[1,128]{1,0:T(1,128)} %param.15) | copy-start | bytes 1540

commit v2 on v1

--- a/solution.py
+++ b/solution.py
@@ -1,3 +1,5 @@
+import functools
+
 import jax
 import jax.numpy as jnp
 from jax import lax
@@ -67,13 +69,14 @@
 MESH = pl.DeviceIdType.MESH
 GRP = 128
 PAD = 128
+ORDER = (3, 0, 2, 1)
 
 
 def fused(
-    tok, gate_hbm, up_hbm, down_hbm, out,
-    held, gate_w, up_w, down_w, hid, scale, part, s_in, f_in, z_in,
+    tok, value_row, seq, gate_hbm, up_hbm, down_hbm, out, rewards,
+    held, gate_w, up_w, down_w, hid, scale, part, s_in, f_in, z_in, stats,
     w_sem, az_s, az_r, af_s, af_r, as_s, as_r, at_s, at_r,
-    rt_s, rt_r, rs_s, rs_r, rf_s, rf_r, rz_s, rz_r,
+    rt_s, rt_r, rs_s, rs_r, rf_s, rf_r, rz_s, rz_r, v_sem,
 ):
     half = out.shape[1]
     t = lax.axis_index("tp")
@@ -125,8 +128,12 @@
     def own_block(d):
         return tok if d == 0 else held.at[t, l_own, span(d)]
 
-    def z_copy(d):
-        return remote(tok, held.at[t, l_own, span(0)], az_s.at[d - 1], az_r.at[d - 1], peer(d))
+    def z_copy(d, step):
+        k = (d + step) % 4
+        return remote(
+            own_block(d), held.at[t, l_own, span(d)], az_s.at[0 if step > 0 else 1, d],
+            az_r.at[k - 1], peer(step % 4),
+        )
 
     def f_copy(d):
         return remote(own_block(d), held.at[t, l_own, span(d)], af_s.at[d], af_r.at[d], near)
@@ -150,21 +157,64 @@
         copy.start()
         sent.append(copy)
 
-    for d in (1, 3, 2):
-        go(z_copy(d))
+    pl.when(z < 3)(lambda: z_copy(0, 1).start())
+    pl.when(z > 0)(lambda: z_copy(0, -1).start())
     go(f_copy(0))
     go(s_copy(0, 0))
     go(t_copy(0, l_own, 0, tok))
     held[t, l_own, span(0)] = tok[...]
-    for d in (0, 1, 3, 2):
-        if d:
-            arrived(l_own, d, az_r.at[d - 1])
-            go(f_copy(d))
-            go(s_copy(0, d))
-            go(t_copy(0, l_own, d))
+
+    def near_block(d):
         arrived(l_f, d, af_r.at[d])
-        go(s_copy(1, d))
-        go(t_copy(i_f, l_f, d))
+        s_copy(1, d).start()
+        t_copy(i_f, l_f, d).start()
+
+    def line_block(d, step):
+        arrived(l_own, d, az_r.at[d - 1])
+        if step > 0 and d < 3:
+            pl.when(z < 3)(lambda: z_copy(d, 1).start())
+        if step < 0 and d > 1:
+            pl.when(z > 0)(lambda: z_copy(d, -1).start())
+        f_copy(d).start()
+        s_copy(0, d).start()
+        t_copy(0, l_own, d).start()
+        near_block(d)
+
+    near_block(0)
+    for hop in (1, 2, 3):
+        pl.when(z >= hop)(functools.partial(line_block, hop, 1))
+        pl.when(z + hop <= 3)(functools.partial(line_block, 4 - hop, -1))
+
+    def gather_sent():
+        for d in range(4):
+            if d < 3:
+                pl.when((z >= d) & (z < 3))(lambda d=d: z_copy(d, 1).wait_send())
+            if d != 1:
+                up = 0 if d == 0 else 4 - d
+                pl.when((z + up <= 3) & (z > 0))(lambda d=d: z_copy(d, -1).wait_send())
+            s_copy(1, d).wait_send()
+            t_copy(i_f, l_f, d).wait_send()
+            if d:
+                f_copy(d).wait_send()
+                s_copy(0, d).wait_send()
+                t_copy(0, l_own, d).wait_send()
+
+    def side(c):
+        return pl.ds(c * (half // 2), half // 2)
+
+    def rows(d):
+        return pl.ds(d * GRP, GRP)
+
+    def rs_copy(k, c, d):
+        i = i_s if k == 0 else 3
+        return remote(
+            part.at[i, rows(d), side(c)], s_in.at[k, rows(d), side(c)],
+            rs_s.at[k, c, d], rs_r.at[k, c, d], far,
+        )
+
+    def send_far(k, c):
+        for d in ORDER:
+            rs_copy(k, c, d).start()
 
     def expert(i):
         line = lines[i]
@@ -175,7 +225,7 @@
         scale[...] = jnp.sum(jnp.where(lax.rem(lane, 16) == e, shares, 0.0), axis=1, keepdims=True)
 
         def hidden(n, carry):
-            cols = pl.ds(pl.multiple_of(n * 256, 256), 256)
+            cols = pl.ds(pl.multiple_of(n * 768, 768), 768)
             a = held[0, line, :, pl.ds(0, half)]
             b = held[1, line, :, pl.ds(0, half)]
             f32 = jnp.float32
@@ -186,23 +236,22 @@
             hid[:, cols] = (g / (1.0 + jnp.exp(-g)) * u * scale[...]).astype(jnp.bfloat16)
             return carry
 
-        lax.fori_loop(0, hid.shape[1] // 256, hidden, 0)
+        lax.fori_loop(0, hid.shape[1] // 768, hidden, 0)
 
         def term(n, core):
-            cols = pl.ds(pl.multiple_of(core * half + n * 256, 256), 256)
+            cols = pl.ds(pl.multiple_of(core * half + n * 512, 512), 512)
             return jnp.dot(hid[...], down_w[:, cols], preferred_element_type=jnp.float32)
 
         def swap(c):
-            cols = pl.ds(c * (half // 2), half // 2)
             return remote(
-                held.at[1 - t, line, :, cols], part.at[i, :, cols],
+                held.at[1 - t, line, :, side(c)], part.at[i, :, side(c)],
                 rt_s.at[i, c], rt_r.at[i, c], twin,
             )
 
-        steps = half // 512
+        steps = half // 1024
         for c in range(2):
             def other(n, carry):
-                cols = pl.ds(pl.multiple_of(n * 256, 256), 256)
+                cols = pl.ds(pl.multiple_of(n * 512, 512), 512)
                 held[1 - t, line, :, cols] = term(n, 1 - t).astype(jnp.bfloat16)
                 return carry
 
@@ -212,20 +261,16 @@
             swap(c).wait_recv()
 
             def mine(n, carry):
-                cols = pl.ds(pl.multiple_of(n * 256, 256), 256)
+                cols = pl.ds(pl.multiple_of(n * 512, 512), 512)
                 total = term(n, t) + part[i, :, cols].astype(jnp.float32)
                 part[i, :, cols] = total.astype(jnp.bfloat16)
                 return carry
 
             lax.fori_loop(c * steps, (c + 1) * steps, mine, 0)
-
-    def rs_copy(k, d):
-        i = i_s if k == 0 else 3
-        return remote(part.at[i, span(d)], s_in.at[k, span(d)], rs_s.at[k, d], rs_r.at[k, d], far)
-
-    def send_far(k):
-        for d in (1, 3, 2, 0):
-            rs_copy(k, d).start()
+            if i == 3:
+                send_far(1, c)
+            elif i > 0:
+                pl.when(t == i - 1)(functools.partial(send_far, 0, c))
 
     for load in loads:
         load.wait()
@@ -234,68 +279,135 @@
         arrived(l_s, d, as_r.at[0, d])
         go(t_copy(i_s, l_s, d))
     expert(1)
-    pl.when(t == 0)(lambda: send_far(0))
     for d in (0, 1, 3, 2):
         arrived(l_diag, d, as_r.at[1, d])
         go(t_copy(3, l_diag, d))
     expert(2)
-    pl.when(t == 1)(lambda: send_far(0))
     expert(3)
-    send_far(1)
-
-    def add(dst, row, *others):
+
+    def add(dst, row, c, *others):
         def chunk(r, carry):
             at = pl.ds(pl.multiple_of(row + r * 16, 16), 16)
-            total = dst[at].astype(jnp.float32)
+            total = dst[at, side(c)].astype(jnp.float32)
             for other in others:
-                total += other[at].astype(jnp.float32)
-            dst[at] = total.astype(jnp.bfloat16)
+                total += other[at, side(c)].astype(jnp.float32)
+            dst[at, side(c)] = total.astype(jnp.bfloat16)
             return carry
 
         lax.fori_loop(0, GRP // 16, chunk, 0)
 
-    def start_row(d):
-        return lax.rem(z - d + 4, 4) * GRP
-
-    def rf_copy(d):
-        return remote(part.at[i_f, span(d)], f_in.at[span(d)], rf_s.at[d], rf_r.at[d], near)
-
-    def rz_copy(d):
+    def rf_copy(c, d):
         return remote(
-            part.at[0, span(d)], z_in.at[d - 1], rz_s.at[d - 1], rz_r.at[d - 1], peer(4 - d)
-        )
-
-    for d in (1, 3, 2, 0):
-        rs_copy(1, d).wait_recv()
-        add(part.at[i_f], start_row(d), s_in.at[1])
-        go(rf_copy(d))
-    for d in (1, 3, 2, 0):
-        rs_copy(0, d).wait_recv()
-        rf_copy(d).wait_recv()
-        add(part.at[0], start_row(d), s_in.at[0], f_in)
-        if d:
-            go(rz_copy(d))
-    for d in (1, 3, 2):
-        rz_copy(d).wait_recv()
+            part.at[i_f, rows(d), side(c)], f_in.at[rows(d), side(c)],
+            rf_s.at[c, d], rf_r.at[c, d], near,
+        )
+
+    def up_copy(c, d):
+        return remote(
+            part.at[0, rows(d), side(c)], z_in.at[0, d - 1, :, side(c)],
+            rz_s.at[0, c, d], rz_r.at[0, c, d], peer(1),
+        )
+
+    def down_copy(c, d):
+        return remote(
+            part.at[0, rows(d), side(c)], z_in.at[1, d, :, side(c)],
+            rz_s.at[1, c, d], rz_r.at[1, c, d], peer(3),
+        )
+
+    def join(way, copy, c, d):
+        copy(c, d).wait_recv()
+        slot = d - 1 if way == 0 else d
+
+        def chunk(r, carry):
+            at = pl.ds(pl.multiple_of(d * GRP + r * 16, 16), 16)
+            came = z_in[way, slot, pl.ds(pl.multiple_of(r * 16, 16), 16), side(c)]
+            total = part[0, at, side(c)].astype(jnp.float32) + came.astype(jnp.float32)
+            part[0, at, side(c)] = total.astype(jnp.bfloat16)
+            return carry
+
+        lax.fori_loop(0, GRP // 16, chunk, 0)
+
+    def line_step(c, d):
+        def up():
+            pl.when(z > 0)(lambda: join(0, up_copy, c, d))
+            up_copy(c, d).start()
+
+        def down():
+            pl.when(z < 3)(lambda: join(1, down_copy, c, d))
+            down_copy(c, d).start()
+
+        if d > 0:
+            pl.when(z < d)(up)
+        if d < 3:
+            pl.when(z > d)(down)
+
+    def line_end(c, d):
+        def mine():
+            if d > 0:
+                join(0, up_copy, c, d)
+            if d < 3:
+                join(1, down_copy, c, d)
+
+        pl.when(z == d)(mine)
+
+    units = [(c, d) for c in range(2) for d in ORDER]
+    for turn in range(len(units) + 1):
+        if turn < len(units):
+            c, d = units[turn]
+            rs_copy(1, c, d).wait_recv()
+            add(part.at[i_f], d * GRP, c, s_in.at[1])
+            go(rf_copy(c, d))
+        if turn > 0:
+            c, d = units[turn - 1]
+            rs_copy(0, c, d).wait_recv()
+            rf_copy(c, d).wait_recv()
+            add(part.at[0], d * GRP, c, s_in.at[0], f_in)
+            line_step(c, d)
+    for c, d in units:
+        line_end(c, d)
+
+    def line_sent():
+        for c, d in units:
+            if d > 0:
+                pl.when(z < d)(lambda c=c, d=d: up_copy(c, d).wait_send())
+            if d < 3:
+                pl.when(z > d)(lambda c=c, d=d: down_copy(c, d).wait_send())
 
     def last(r, carry):
         at = pl.ds(pl.multiple_of(r * 16, 16), 16)
         total = part[0, pl.ds(pl.multiple_of(z * GRP + r * 16, 16), 16)].astype(jnp.float32)
-        for k in range(3):
-            total += z_in[k, at].astype(jnp.float32)
         total += tok[at, pl.ds(0, half)].astype(jnp.float32)
-        out[at] = total.astype(jnp.bfloat16)
+        rounded = total.astype(jnp.bfloat16)
+        out[at] = rounded
+        as_float = rounded.astype(jnp.float32)
+        squares = jnp.sum(as_float * as_float, axis=1, keepdims=True)
+        along = jnp.sum(as_float * value_row[...], axis=1, keepdims=True)
+        lane = lax.broadcasted_iota(jnp.int32, (16, PAD), 1)
+        stats[0, at] = jnp.where(lane == 0, squares, along)
         return carry
 
     lax.fori_loop(0, GRP // 16, last, 0)
+    trade = remote(stats.at[0], stats.at[1], v_sem.at[0], v_sem.at[1], twin)
+    trade.start()
     for copy in sent:
         copy.wait_send()
+    gather_sent()
+    line_sent()
     for k in range(2):
-        for d in range(4):
-            rs_copy(k, d).wait_send()
-
-
-def routed_layer(block, gate, up, down):
+        for c in range(2):
+            for d in range(4):
+                rs_copy(k, c, d).wait_send()
+    trade.wait()
+    both = stats[0] + stats[1]
+    values = both[:, 1:2] * lax.rsqrt(both[:, 0:1] / (2 * half) + 1e-06)
+    lane = lax.broadcasted_iota(jnp.int32, (GRP, PAD), 1)
+    members = (seq[...] == lane).astype(jnp.float32)
+    sums = jnp.sum(members * values, axis=0, keepdims=True)
+    counts = jnp.sum(members, axis=0, keepdims=True)
+    rewards[...] = sums / jnp.maximum(counts, 1.0)
+
+
+def routed_layer(block, value_row, seq, gate, up, down):
     half = block.shape[1] - PAD
     width, units = gate.shape
     bf16 = jnp.bfloat16
@@ -303,9 +415,12 @@
     flops = 2 * 16 * GRP * 3 * width * units
     return pl.pallas_call(
         fused,
-        out_shape=jax.ShapeDtypeStruct((GRP, half), bf16),
-        in_specs=[pl.BlockSpec(memory_space=pltpu.VMEM)] + [pl.BlockSpec(memory_space=pl.ANY)] * 3,
-        out_specs=pl.BlockSpec(memory_space=pltpu.VMEM),
+        out_shape=(
+            jax.ShapeDtypeStruct((GRP, half), bf16),
+            jax.ShapeDtypeStruct((1, PAD), jnp.float32),
+        ),
+        in_specs=[pl.BlockSpec(memory_space=pltpu.VMEM)] * 3 + [pl.BlockSpec(memory_space=pl.ANY)] * 3,
+        out_specs=(pl.BlockSpec(memory_space=pltpu.VMEM),) * 2,
         scratch_shapes=[
             pltpu.VMEM((2, 4, 4 * GRP, half + PAD), bf16),
             pltpu.VMEM((width, units), bf16),
@@ -316,16 +431,18 @@
             pltpu.VMEM((4, 4 * GRP, half), bf16),
             pltpu.VMEM((2, 4 * GRP, half), bf16),
             pltpu.VMEM((4 * GRP, half), bf16),
-            pltpu.VMEM((3, GRP, half), bf16),
+            pltpu.VMEM((2, 3, GRP, half), bf16),
+            pltpu.VMEM((2, GRP, PAD), jnp.float32),
             dma((3,)),
-            dma((3,)), dma((3,)),
+            dma((2, 4)), dma((3,)),
             dma((4,)), dma((4,)),
             dma((2, 4)), dma((2, 4)),
             dma((4, 4)), dma((4, 4)),
             dma((4, 2)), dma((4, 2)),
+            dma((2, 2, 4)), dma((2, 2, 4)),
             dma((2, 4)), dma((2, 4)),
-            dma((4,)), dma((4,)),
-            dma((3,)), dma((3,)),
+            dma((2, 2, 4)), dma((2, 2, 4)),
+            dma((2,)),
         ],
         compiler_params=pltpu.CompilerParams(
             collective_id=0, has_side_effects=True, vmem_limit_bytes=63 * 1024 * 1024
@@ -333,7 +450,7 @@
         cost_estimate=pl.CostEstimate(
             flops=flops, bytes_accessed=6 * width * units, transcendentals=16 * GRP * units
         ),
-    )(block, gate, up, down)
+    )(block, value_row, seq, gate, up, down)
 
 
 def shards(
@@ -348,7 +465,6 @@
 ):
     tok_count, width_part = tokens.shape
     groups = lax.axis_size("ep")
-    parts = lax.axis_size("tp")
     share = route_weights / jnp.sum(route_weights, axis=1, keepdims=True)
     named = expert_ids[:, :, None] == jnp.arange(groups, dtype=jnp.int32)[None, None, :]
     dense = jnp.sum(jnp.where(named, share[:, :, None], 0.0), axis=1)
@@ -360,8 +476,11 @@
         rest = rest - top
     blank = jnp.zeros((tok_count, PAD - 3 * groups), jnp.bfloat16)
     block = jnp.concatenate([tokens] + columns + [blank], axis=1)
-    layer_output = routed_layer(block, gate_weight[0], up_weight[0], down_weight[0])
-    return (layer_output, head(layer_output, value_weight, sequence_ids, parts))
+    layer_output, rewards = routed_layer(
+        block, value_weight[None, :], sequence_ids.reshape(tok_count, 1),
+        gate_weight[0], up_weight[0], down_weight[0],
+    )
+    return (layer_output, rewards[:, :SEQ_GRP])
 
 
 def solution(mesh):

time: 232 us -> 216 us (0.931)
  blocking collectives: 10.3 us -> 0 us
  Pallas kernels: 213 us -> 206 us
  local copies, waits for them, and re-layouts: 4.06 us -> 6.58 us
    psum x1 -> x0, blocking collectives: 10.3 us -> none  [head(): squares, along = lax.psum((squares, along), 'tp')]
    pallas_call x1, Pallas kernels: 213 us -> 206 us  [routed_layer(): pl.pallas_call(fused, out_shape=(jax.ShapeDtypeStruct((GRP, half), bf16),...]
where the time goes in v2:
time: 216 us; the launch traced here: 215 us
  Pallas kernels  206 us (95%)
  local copies, waits for them, and re-layouts  6.58 us (3%)
    pallas_call x1, Pallas kernels, routed_layer(): pl.pallas_call(fused, out_shape=(jax.ShapeDtypeStruct((GRP, half), bf16),...  206 us

profile of v2, /device:TPU:0, one launch (start us, length us, event | category | flops | bytes accessed | tf_op | source)
XLA Modules:
  0.0 214.9 jit_solution(7665463994162920174)
XLA Ops:
  0.6 0.7 reduce_sum.18
  1.3 0.7 broadcast_divide_fusion
  2.0 0.7 select_reduce_fusion
  2.7 0.1 copy.18
  2.9 0.1 copy.17
  3.0 0.1 copy.16
  3.1 1.4 copy.19.seq
  4.5 1.8 concatenate.3.tok
  6.3 205.6 %shard_map.95 = (bf16[128,2048]{1,0:T(8,128)(2,1)}, f32[1,128]{1,0:T(1,128)}) custom-call(bf16[128,2176]{1,0:T(8,128)(2,1)} %concatenate.3.tok, f32[1,2048]{1,0:T(1,128)} %bitcast.10, s32[128,1]{1,0:T(8,128)} %copy.19.seq, bf16[4096,768]{1,0:T(8,128)(2,1)} %bitcast.7, bf16[4096,768]{1,0:T(8,128)(2,1)} %bitcast.8, bf16[768,4096]{1,0:T(8,128)(2,1)} %bitcast.9), custom_call_target="tpu_custom_call" | custom-call | flops 38654705664 | bytes 18874368 | tf_op jit(solution)/shard_map/pallas_call | solution.py:416
  211.9 1.9 copy.22
  213.8 1.1 copy.23
  (3 shorter events, 0.0 us)
